TPU v7x, 256 devices: a whole 4x4x8 slice. The times are simulated.
256 devices in a mesh: seq: 16 (over z, core), head: 16 (over y, x).
Axes of the slice: x: 4, y: 4, z: 8, core: 2. Of those that a mesh axis runs over, the one named last changes fastest.
Arguments:
- queries: bfloat16 [6144, 16384], P('seq', 'head'), may hold values from -5 to 5
- keys: bfloat16 [6144, 1024], P('seq', 'head'), may hold values from -5 to 5
- values: bfloat16 [6144, 1024], P('seq', 'head'), may hold values from -6 to 6
- feat_q: bfloat16 [128, 128, 128], P('head'), may hold values from -0.5 to 0.5
- feat_k: bfloat16 [128, 128, 128], P('head'), may hold values from -0.5 to 0.5
Outputs:
- grad_feat_q: float32 [128, 128, 128], P('head')
- grad_feat_k: float32 [128, 128, 128], P('head')
All inputs are finite; a program needn't handle non-finite values.
Results may differ from a plain program's by a relative error of at most 0.02.
Values may be sent and summed in bfloat16 or wider, within the bound.
A program may use at most 128 MiB of HBM per device.

v0:
```python
import math
import jax
import jax.numpy as jnp
from jax import lax
from jax.sharding import PartitionSpec as P

HIGHEST_MODE = lax.Precision.HIGHEST
MASKED_SCORE = -1e30


def from_partner(block, axis, stride):
    count = lax.axis_size(axis)
    route = []
    for low in range(count):
        high = low | 1 << stride
        if high != low and high < count:
            route += [(low, high), (high, low)]
    return lax.ppermute(block, axis, route)


def in_one_piece(arrays, axis, dim, along):
    columns = [a.reshape(*a.shape[:along], -1) for a in arrays]
    both = jnp.concatenate(columns, axis=along)
    filled, at, done = (lax.all_gather(both, axis, axis=dim, tiled=True), 0, [])
    for a, column in zip(arrays, columns):
        piece = filled[..., at : at + column.shape[along]]
        done.append(piece.reshape(*piece.shape[:along], *a.shape[along:]))
        at += column.shape[along]
    return tuple(done)


def together(arrays, axis):
    vector, at, done = (jnp.concatenate([a.reshape(-1) for a in arrays]), 0, [])
    so_far = lax.psum(vector, axis)
    for a in arrays:
        done.append(so_far[at : at + a.size].reshape(a.shape))
        at += a.size
    return tuple(done)


def split_wide(entries):
    high = entries.astype(jnp.bfloat16)
    low = (entries - high.astype(jnp.float32)).astype(jnp.bfloat16)
    return (high, low)


def wide_left(form, wide, narrow):
    high, low = split_wide(wide)
    return jnp.einsum(form, high, narrow, preferred_element_type=jnp.float32) + jnp.einsum(
        form, low, narrow, preferred_element_type=jnp.float32
    )


def wide_right(form, narrow, wide):
    high, low = split_wide(wide)
    return jnp.einsum(form, narrow, high, preferred_element_type=jnp.float32) + jnp.einsum(
        form, narrow, low, preferred_element_type=jnp.float32
    )


def attend_block(
    running, query_half, query_pos, key_rows, value_rows, key_first, group_count, score_scale
):
    row_peak, row_total, summed = running
    half_rows = query_half.shape[0]
    key_count = key_rows.shape[0]
    head_dim = key_rows.shape[1] // group_count
    grouped = query_half.reshape(half_rows, group_count, -1, head_dim)
    key_heads = key_rows.reshape(key_count, group_count, head_dim)
    value_heads = value_rows.reshape(key_count, group_count, head_dim)
    scores = (
        jnp.einsum("rgjd,kgd->gjrk", grouped, key_heads, preferred_element_type=jnp.float32)
        * score_scale
    )
    scores = scores.reshape(row_peak.shape[0], half_rows, key_count)
    key_pos = key_first + jnp.arange(key_count, dtype=jnp.int32)
    allowed = (key_pos[None, :] <= query_pos[:, None])[None]
    new_peak = jnp.maximum(row_peak, jnp.max(jnp.where(allowed, scores, MASKED_SCORE), axis=-1))
    weights = jnp.exp(jnp.where(allowed, scores - new_peak[..., None], MASKED_SCORE))
    factor = jnp.exp(row_peak - new_peak)
    row_total = row_total * factor + jnp.sum(weights, axis=-1)
    rounded = weights.astype(jnp.bfloat16).reshape(group_count, -1, half_rows, key_count)
    mixture = jnp.einsum("gjrk,kgd->gjrd", rounded, value_heads, preferred_element_type=jnp.float32)
    summed = summed * factor[..., None] + mixture.reshape(summed.shape)
    return (new_peak, row_total, summed)


def body(queries, keys, values, feat_q, feat_k):
    row_count = queries.shape[0]
    heads_here = feat_q.shape[0]
    head_dim = feat_q.shape[1]
    seq_count = lax.axis_size("seq")
    seq_place = lax.axis_index("seq")
    head_place = lax.axis_index("head")
    key_value = jnp.stack((keys, values))
    partner = from_partner(key_value, "head", 0)
    upper_half = head_place // (1 << 0) % 2 == 1
    key_value = jnp.where(
        upper_half,
        jnp.concatenate((partner, key_value), axis=2),
        jnp.concatenate((key_value, partner), axis=2),
    )
    group_count = key_value.shape[2] // head_dim
    group_size = heads_here // group_count
    query_pos = seq_place * row_count + jnp.arange(row_count, dtype=jnp.int32)
    half_rows = row_count // 2
    query_halves = (queries[:half_rows], queries[half_rows:])
    pos_halves = (query_pos[:half_rows], query_pos[half_rows:])
    top_halves = (jnp.max(pos_halves[0]), jnp.max(pos_halves[1]))
    score_scale = head_dim ** (-0.5)
    start_half = (
        jnp.full((heads_here, half_rows), MASKED_SCORE, jnp.float32),
        jnp.zeros((heads_here, half_rows), jnp.float32),
        jnp.zeros((heads_here, half_rows, head_dim), jnp.float32),
    )
    shard_part = lax.all_gather(key_value, "seq", axis=1, tiled=True)
    part_rows = shard_part.shape[1]
    block_rows = math.gcd(part_rows, 512)

    def one_step(step_index, halves_state):
        offset = step_index * block_rows
        key_rows = lax.dynamic_slice_in_dim(shard_part[0], offset, block_rows, 0)
        value_rows = lax.dynamic_slice_in_dim(shard_part[1], offset, block_rows, 0)
        updated = []
        for half_index in range(2):

            def attend_half(current, half_index=half_index):
                return attend_block(
                    current,
                    query_halves[half_index],
                    pos_halves[half_index],
                    key_rows,
                    value_rows,
                    offset,
                    group_count,
                    score_scale,
                )

            def unchanged(current):
                return current

            updated.append(
                lax.cond(
                    top_halves[half_index] >= offset,
                    attend_half,
                    unchanged,
                    halves_state[half_index],
                )
            )
        return tuple(updated)

    finished = lax.fori_loop(0, part_rows // block_rows, one_step, (start_half, start_half))
    teacher_out = jnp.concatenate(
        [
            (finished[half_index][2] / finished[half_index][1][..., None]).astype(jnp.bfloat16)
            for half_index in range(2)
        ],
        axis=1,
    )
    key_local = key_value[0].reshape(row_count, group_count, head_dim)
    value_local = key_value[1].reshape(row_count, group_count, head_dim)
    query_local = queries.reshape(row_count, heads_here, head_dim)
    query_pre = jnp.einsum("rhd,hdf->hrf", query_local, feat_q, preferred_element_type=jnp.float32)
    key_pre = jnp.einsum(
        "rgd,gjdf->gjrf",
        key_local,
        feat_k.reshape(group_count, group_size, head_dim, -1),
        preferred_element_type=jnp.float32,
    ).reshape(heads_here, row_count, -1)
    feat_count = query_pre.shape[-1]
    query_feat = jax.nn.softplus(query_pre).astype(jnp.bfloat16)
    key_feat = jax.nn.softplus(key_pre).astype(jnp.bfloat16)
    block_state = jnp.einsum(
        "gjrf,rgd->gjfd",
        key_feat.reshape(group_count, group_size, row_count, -1),
        value_local,
        preferred_element_type=jnp.float32,
    ).reshape(heads_here, feat_count, head_dim)
    block_norm = jnp.sum(key_feat, axis=1, dtype=jnp.float32)
    zero_pair = (jnp.zeros_like(block_state), jnp.zeros_like(block_norm))
    take_shard_part = tuple(
        (
            part.astype(jnp.float32)
            for part in in_one_piece(
                (block_state[None].astype(jnp.bfloat16), block_norm[None].astype(jnp.bfloat16)),
                "seq",
                0,
                3,
            )
        )
    )
    part_count = take_shard_part[0].shape[0]
    chosen = jnp.arange(part_count, dtype=jnp.int32) < seq_place
    before_state = zero_pair[0] + jnp.sum(
        jnp.where(chosen[:, None, None, None], take_shard_part[0], 0.0), axis=0
    )
    before_norm = zero_pair[1] + jnp.sum(
        jnp.where(chosen[:, None, None], take_shard_part[1], 0.0), axis=0
    )
    causal = jnp.arange(row_count)[:, None] >= jnp.arange(row_count)[None, :]
    affinity = jnp.einsum("hrf,hsf->hrs", query_feat, key_feat, preferred_element_type=jnp.float32)
    masked = jnp.where(causal[None], affinity, 0.0)
    local_mix = jnp.einsum(
        "gjrs,sgd->gjrd",
        masked.astype(jnp.bfloat16).reshape(group_count, group_size, row_count, row_count),
        value_local,
        preferred_element_type=jnp.float32,
    ).reshape(heads_here, row_count, head_dim)
    numerator = wide_right("hrf,hfd->hrd", query_feat, before_state) + local_mix
    denominator = wide_right("hrf,hf->hr", query_feat, before_norm) + jnp.sum(masked, axis=-1)
    student = numerator / denominator[..., None]
    total_tokens = row_count * seq_count
    grad_out = 2.0 * (student - teacher_out.astype(jnp.float32)) / total_tokens
    grad_numer = grad_out / denominator[..., None]
    grad_denom = -jnp.sum(grad_out * student, axis=-1) / denominator
    back_state = wide_right("hrf,hrd->hfd", query_feat, grad_numer)
    back_norm = wide_right("hrf,hr->hf", query_feat, grad_denom)

    def take_upper(running, shard_part):
        part_count = shard_part[0].shape[0]
        chosen = jnp.arange(part_count, dtype=jnp.int32) > seq_place
        return (
            running[0]
            + jnp.sum(jnp.where(chosen[:, None, None, None], shard_part[0], 0.0), axis=0),
            running[1] + jnp.sum(jnp.where(chosen[:, None, None], shard_part[1], 0.0), axis=0),
        )

    after_state, after_norm = take_upper(
        zero_pair,
        (
            lax.all_gather(back_state[None].astype(jnp.bfloat16), "seq", axis=0, tiled=True).astype(
                jnp.float32
            ),
            lax.all_gather(back_norm[None].astype(jnp.bfloat16), "seq", axis=0, tiled=True).astype(
                jnp.float32
            ),
        ),
    )
    grad_aff = wide_left(
        "gjrd,sgd->gjrs",
        grad_numer.reshape(group_count, group_size, row_count, head_dim),
        value_local,
    ).reshape(heads_here, row_count, row_count)
    grad_aff = jnp.where(causal[None], grad_aff + grad_denom[..., None], 0.0)
    grad_qfeat = (
        jnp.einsum("hrd,hfd->hrf", grad_numer, before_state, precision=HIGHEST_MODE)
        + grad_denom[..., None] * before_norm[:, None, :]
        + wide_left("hrs,hsf->hrf", grad_aff, key_feat)
    )
    grad_kfeat = (
        wide_right(
            "sgd,gjfd->gjsf",
            value_local,
            after_state.reshape(group_count, group_size, feat_count, head_dim),
        ).reshape(heads_here, row_count, feat_count)
        + after_norm[:, None, :]
        + wide_left("hrs,hrf->hsf", grad_aff, query_feat)
    )
    grad_wq = wide_right("rhd,hrf->hdf", query_local, grad_qfeat * jax.nn.sigmoid(query_pre))
    grad_wk = wide_right(
        "rgd,gjrf->gjdf",
        key_local,
        (grad_kfeat * jax.nn.sigmoid(key_pre)).reshape(
            group_count, group_size, row_count, feat_count
        ),
    ).reshape(heads_here, head_dim, feat_count)
    return tuple(
        (
            part.astype(jnp.float32)
            for part in together(
                (grad_wq.astype(jnp.bfloat16), grad_wk.astype(jnp.bfloat16)), "seq"
            )
        )
    )


def solution(mesh):
    return jax.shard_map(
        body,
        mesh=mesh,
        in_specs=(
            P("seq", "head"),
            P("seq", "head"),
            P("seq", "head"),
            P("head", None, None),
            P("head", None, None),
        ),
        out_specs=(P("head", None, None), P("head", None, None)),
        check_vma=False,
    )
```

profile of v0, /device:TPU:1, one launch (start us, length us, event | category | flops | bytes accessed | tf_op | source)
XLA Modules:
  0.0 392.3 jit_solution(10411164082974506304)
XLA Ops:
  9.3 2.1 collective-permute-start
  11.4 3.4 collective-permute-done
  21.4 2.2 select_reduce_fusion.1
  23.7 38.1 %all-gather.8.cloned.1.call-done = bf16[2,6144,128]{2,1,0:T(8,128)(2,1)} async-done(((bf16[2,384,128]{2,1,0:T(8,128)(2,1)}), bf16[2,6144,128]{2,1,0:T(8,128)(2,1)}) %all-gather.8.cloned.1.call-update) | async-done | bytes 3145744 | tf_op jit(solution)/shard_map/all_gather | solution.py:116
  62.8 56.6 %while.23 = (s32[]{:T(128)}, f32[8,192]{1,0:T(8,128)S(1)}, f32[8,192]{1,0:T(8,128)S(1)}, f32[8,192,128]{2,1,0:T(8,128)}, f32[8,192]{1,0:T(8,128)S(1)}, /*index=5...) while((s32[]{:T(128)}, f32[8,192]{1,0:T(8,128)S(1)}, ...), condition=%wide.region_15.16_spmd, body=%wide.region_6.15_spmd.sunk | while | flops 823598080 | bytes 37431328 | solution.py:152
  64.0 2.1 fusion.153
  66.2 4.4 %conditional.4 = ((f32[8,192]{1,0:T(8,128)S(1)}, f32[8,192]{1,0:T(8,128)S(1)}, f32[8,192,128]{2,1,0:T(8,128)})) conditional(s32[]{:T(128)} %convert_element_type.400, (f32[8,192]{1,0:T(8,128)S(1)}, f32[8,192]{1,0:T(8,128)S(1)}, f32[8,192,128]{2,1,0:T(8,128)}) %tuple.74, (s32[]{:T(128)}, s32[192]{0:T(256)S(1)}, bf16[192,1024]{1,0:T(8,128)(2,1)S(1)}, ...), branch_computations={%region_7.7_spmd, %region_8.10_spmd} | conditional | flops 411799040 | bytes 18453340 | solution.py:143
  70.6 3.5 conditional.5
  75.3 2.1 fusion.153
  77.4 4.4 %conditional.4 = ((f32[8,192]{1,0:T(8,128)S(1)}, f32[8,192]{1,0:T(8,128)S(1)}, f32[8,192,128]{2,1,0:T(8,128)})) conditional(s32[]{:T(128)} %convert_element_type.400, (f32[8,192]{1,0:T(8,128)S(1)}, f32[8,192]{1,0:T(8,128)S(1)}, f32[8,192,128]{2,1,0:T(8,128)}) %tuple.74, (s32[]{:T(128)}, s32[192]{0:T(256)S(1)}, bf16[192,1024]{1,0:T(8,128)(2,1)S(1)}, ...), branch_computations={%region_7.7_spmd, %region_8.10_spmd} | conditional | flops 411799040 | bytes 18453340 | solution.py:143
  81.9 3.5 conditional.5
  86.6 2.1 fusion.153
  90.0 2.2 fusion.153
  93.5 2.1 fusion.153
  96.9 2.1 fusion.153
  100.3 2.1 fusion.153
  103.7 2.1 fusion.153
  107.1 2.1 fusion.153
  110.5 2.1 fusion.153
  113.9 2.1 fusion.153
  121.8 2.5 copy.124
  124.3 2.4 divide_convert_fusion
  126.7 4.6 %slice.72 = bf16[16,8,128,128]{2,1,3,0:T(8,128)(2,1)} slice(bf16[16,8,128,129]{2,1,3,0:T(8,128)(2,1)} %all-gather.6.cloned.1.call-done), slice={[0:16], [0:8], [0:128], [0:128]} | slice | bytes 8388608 | tf_op jit(solution)/shard_map/slice | solution.py:26
  131.2 6.7 %copy.186 = bf16[16,8,128,128]{3,2,1,0:T(8,128)(2,1)} copy(bf16[16,8,128,128]{2,1,3,0:T(8,128)(2,1)} %slice.72) | data formatting | bytes 8388608
  137.9 3.2 select_reduce_fusion
  147.3 2.8 fusion.128
  158.5 91.9 %all-gather.1 = bf16[128,128]{1,0:T(8,128)(2,1)S(1)} all-gather(bf16[8,128]{1,0:T(8,128)(2,1)S(1)} %add_convert_fusion), channel_id=3, replica_groups=mesh['seq'=16,'head'=16] {'seq'}, dimensions={0}, use_global_device_ids=true | all-gather | bytes 34816 | tf_op jit(solution)/shard_map/all_gather | solution.py:234
  250.5 4.7 %fusion.117 = f32[8,384,128]{2,1,0:T(8,128)S(1)} fusion(bf16[8,384,128]{2,1,0:T(8,128)(2,1)S(1)} %select_convert_fusion.2, f32[8,384,384]{1,2,0:T(8,128)} %copy-done.2), kind=kOutput, calls=%fused_computation.179 | convolution fusion | flops 306708480 | bytes 7077888 | tf_op jit(solution)/shard_map/hrs,hrf->hsf/dot_general | solution.py:49
  257.2 7.9 %all-gather.10.cloned.1.call-done = bf16[128,128,128]{2,1,0:T(8,128)(2,1)} async-done(((bf16[8,128,128]{2,1,0:T(8,128)(2,1)}), bf16[128,128,128]{2,1,0:T(8,128)(2,1)}) %all-gather.10.cloned.1.call-update) | async-done | bytes 4194320 | tf_op jit(solution)/shard_map/all_gather | solution.py:231
  265.1 3.2 fusion.48
  269.9 2.1 fusion.55
  274.2 108.8 %all-reduce.2.cloned.1.call-done = bf16[262144]{0:T(1024)(128)(2,1)} async-done(((bf16[262144]{0:T(1024)(128)(2,1)}), bf16[262144]{0:T(1024)(128)(2,1)}) %all-reduce.2.cloned.1.call-update) | async-done | bytes 524304 | tf_op jit(solution)/shard_map/psum | solution.py:34
  (181 shorter events, 53.4 us)
Async XLA Ops:
  7.2 10.8 %copy-start = (bf16[8,128,128]{2,1,0:T(8,128)(2,1)S(1)}, bf16[8,128,128]{2,1,0:T(8,128)(2,1)}, u32[]{:S(2)}) copy-start(bf16[8,128,128]{2,1,0:T(8,128)(2,1)} %param.15) | copy-start | bytes 786436
  7.2 9.3 %copy-start.5 = (bf16[384,1024]{1,0:T(8,128)(2,1)S(1)}, bf16[384,1024]{1,0:T(8,128)(2,1)}, u32[]{:S(2)}) copy-start(bf16[384,1024]{1,0:T(8,128)(2,1)} %param.11) | copy-start | bytes 2359300
  7.2 54.6 %all-gather.8.cloned.1.call-start = ((), (), s32[]{:S(2)}) async-start(), calls=%async_computation.1 | async-start | bytes 3342336 | tf_op jit(solution)/shard_map/all_gather | solution.py:116
  8.2 8.3 %copy-start.18 = (bf16[8,128,128]{2,1,0:T(8,128)(2,1)S(1)}, bf16[8,128,128]{2,1,0:T(8,128)(2,1)}, u32[]{:S(2)}) copy-start(bf16[8,128,128]{2,1,0:T(8,128)(2,1)} %param.14) | copy-start | bytes 786436
  9.3 5.5 %collective-permute-start = (bf16[2,384,64]{2,1,0:T(8,128)(2,1)S(1)}, bf16[2,384,64]{2,1,0:T(8,128)(2,1)S(1)}, u32[]{:S(2)}, u32[]{:S(2)}) collective-permute-start(bf16[2,384,64]{2,1,0:T(8,128)(2,1)S(1)} %pad_maximum_fusion.3), channel_id=1, source_target_pairs={{0,1},{1,0},{2,3},{3,2},{4,5},{5,4},{6,7},{7,6},{8,9},{9,8},{10,11... | collective-permute-start | bytes 294920 | tf_op jit(solution)/shard_map/ppermute | solution.py:18
  15.7 111.0 %all-gather.6.cloned.1.call-start = ((), (), s32[]{:S(2)}) async-start(), calls=%async_computation | async-start | bytes 4491264 | tf_op jit(solution)/shard_map/all_gather | solution.py:24
  17.0 2.2 copy-start.3
  17.0 1.1 copy-start.8
  19.2 1.2 copy-start.14
  19.2 2.2 copy-start.9
  21.2 243.9 %all-gather.10.cloned.1.call-start = ((), (), s32[]{:S(2)}) async-start(), calls=%async_computation.3 | async-start | bytes 4456448 | tf_op jit(solution)/shard_map/all_gather | solution.py:231
  67.1 1.1 copy-start.12
  69.7 0.9 copy-start.13
  78.4 1.2 copy-start.12
  81.0 0.9 copy-start.13
  119.5 0.9 copy-start.11
  141.8 2.4 copy-start.19
  142.2 1.9 copy-start.16
  142.3 1.9 copy-start.17
  147.0 236.0 %all-reduce.2.cloned.1.call-start = ((), (), s32[]{:S(2)}) async-start(), calls=%async_computation.2 | async-start | bytes 1048576 | tf_op jit(solution)/shard_map/psum | solution.py:34
  150.8 1.1 copy-start.10
  152.0 2.1 copy-start.2
  152.0 2.5 copy-start.4
  154.5 1.7 copy-start.6
  156.2 99.0 %slice-start = ((s8[4718592]{0:T(1024)(128)(4,1)}), s8[524288]{0:T(1024)(128)(4,1)S(1)}, s32[]{:S(2)}) async-start(s8[4718592]{0:T(1024)(128)(4,1)} %bitcast.271), calls=%async_computation.4 | async-start | bytes 1048576
  158.2 97.0 %slice-start.1 = ((s8[4718592]{0:T(1024)(128)(4,1)}), s8[4194304]{0:T(1024)(128)(4,1)S(1)}, s32[]{:S(2)}) async-start(s8[4718592]{0:T(1024)(128)(4,1)} %bitcast.271), calls=%async_computation.5 | async-start | bytes 8388608
  268.5 1.4 copy-start.7
  272.4 1.0 copy-start.15
  274.2 111.6 %copy-start.1 = (bf16[8,128,128]{2,1,0:T(8,128)(2,1)S(1)}, bf16[8,128,128]{2,1,0:T(8,128)(2,1)}, u32[]{:S(2)}) copy-start(bf16[8,128,128]{2,1,0:T(8,128)(2,1)} %param.15) | copy-start | bytes 786436
Sparse Core Ops, SparseCore 0:
  15.8 45.9 all-gather.7
  63.7 40.6 all-gather.5
  147.1 117.8 all-gather.9
  274.3 108.6 all-reduce.1
where the time goes:
time: 394 us; the launch traced here: 392 us
  waiting for transfers between devices  158 us (40%)
  blocking collectives  91.9 us (23%)
  local copies, waits for them, and re-layouts  53.3 us (14%)
  matrix products  36.4 us (9%)
  other arithmetic  20.1 us (5%)
  loops' own time  15.4 us (4%)
  between operations  14.2 us (4%)
    psum x1, waiting for transfers between devices, together(): so_far = lax.psum(vector, axis)  109 us
    all_gather x1, blocking collectives, body(): lax.all_gather(back_norm[None].astype(jnp.bfloat16), 'seq', axis=0, tiled...  91.9 us
    all_gather x1, waiting for transfers between devices, body(): shard_part = lax.all_gather(key_value, 'seq', axis=1, tiled=True)  38.1 us
    slice x12, local copies, waits for them, and re-layouts, one_step(): value_rows = lax.dynamic_slice_in_dim(shard_part[1], offset, block_rows, 0)  25.2 us
    another operation x1, loops' own time, body(): lax.fori_loop(0, part_rows // block_rows, one_step, (start_half, start_ha...  14.8 us
    unnamed x45, local copies, waits for them, and re-layouts  13.5 us
  transfers between devices with their start and end apart: 5, of which 4 were waited for; matrix products, arithmetic and copies ran while one was open for 18% of the time, Pallas kernels for 0%

commit v1 on v0

--- a/solution.py
+++ b/solution.py
@@ -31,7 +31,7 @@
 
 def together(arrays, axis):
     vector, at, done = (jnp.concatenate([a.reshape(-1) for a in arrays]), 0, [])
-    so_far = lax.psum(vector, axis)
+    so_far = jnp.sum(lax.all_gather(vector, axis), axis=0)
     for a in arrays:
         done.append(so_far[at : at + a.size].reshape(a.shape))
         at += a.size

time: 394 us -> 358 us (0.909)
  waiting for transfers between devices: 158 us -> 103 us
  other arithmetic: 20.1 us -> 32.1 us
  local copies, waits for them, and re-layouts: 53.3 us -> 59.9 us
    psum x1 -> x0, waiting for transfers between devices: 109 us -> none  [together(): so_far = lax.psum(vector, axis)]
    all_gather x0 -> x1, waiting for transfers between devices: none -> 54.6 us  [together(): so_far = jnp.sum(lax.all_gather(vector, axis), axis=0)]
    reduce_sum x0 -> x1, other arithmetic: none -> 11.9 us  [together(): so_far = jnp.sum(lax.all_gather(vector, axis), axis=0)]
    all_gather x0 -> x1, local copies, waits for them, and re-layouts: none -> 7.63 us  [together(): so_far = jnp.sum(lax.all_gather(vector, axis), axis=0)]
  transfers between devices with their start and end apart: 5 -> 5, of which waited for: 4 -> 4; matrix products, arithmetic and copies ran while one was open for 18% -> 20% of each run, Pallas kernels for 0% -> 0%
where the time goes in v1:
time: 358 us; the launch traced here: 357 us
  waiting for transfers between devices  103 us (29%)
  blocking collectives  92.6 us (26%)
  local copies, waits for them, and re-layouts  59.9 us (17%)
  matrix products  36.4 us (10%)
  other arithmetic  32.1 us (9%)
  loops' own time  15.4 us (4%)
  between operations  14.2 us (4%)
    all_gather x1, blocking collectives, body(): lax.all_gather(back_norm[None].astype(jnp.bfloat16), 'seq', axis=0, tiled...  92.6 us
    all_gather x1, waiting for transfers between devices, together(): so_far = jnp.sum(lax.all_gather(vector, axis), axis=0)  54.6 us
    all_gather x1, waiting for transfers between devices, body(): shard_part = lax.all_gather(key_value, 'seq', axis=1, tiled=True)  38.1 us
    slice x12, local copies, waits for them, and re-layouts, one_step(): value_rows = lax.dynamic_slice_in_dim(shard_part[1], offset, block_rows, 0)  25.2 us
    another operation x1, loops' own time, body(): lax.fori_loop(0, part_rows // block_rows, one_step, (start_half, start_ha...  14.8 us
    unnamed x45, local copies, waits for them, and re-layouts  13.5 us
    reduce_sum x1, other arithmetic, together(): so_far = jnp.sum(lax.all_gather(vector, axis), axis=0)  11.9 us
    all_gather x1, local copies, waits for them, and re-layouts, together(): so_far = jnp.sum(lax.all_gather(vector, axis), axis=0)  7.63 us
  transfers between devices with their start and end apart: 5, of which 4 were waited for; matrix products, arithmetic and copies ran while one was open for 20% of the time, Pallas kernels for 0%

profile of v1, /device:TPU:1, one launch (start us, length us, event | category | flops | bytes accessed | tf_op | source)
XLA Modules:
  0.0 356.6 jit_solution(12838883534251940371)
XLA Ops:
  9.3 2.1 collective-permute-start
  11.4 3.4 collective-permute-done
  21.4 2.2 select_reduce_fusion.1
  23.7 38.1 %all-gather.10.cloned.1.call-done = bf16[2,6144,128]{2,1,0:T(8,128)(2,1)} async-done(((bf16[2,384,128]{2,1,0:T(8,128)(2,1)}), bf16[2,6144,128]{2,1,0:T(8,128)(2,1)}) %all-gather.10.cloned.1.call-update) | async-done | bytes 3145744 | tf_op jit(solution)/shard_map/all_gather | solution.py:116
  62.8 56.6 %while.23 = (s32[]{:T(128)}, f32[8,192]{1,0:T(8,128)S(1)}, f32[8,192]{1,0:T(8,128)S(1)}, f32[8,192,128]{2,1,0:T(8,128)}, f32[8,192]{1,0:T(8,128)S(1)}, /*index=5...) while((s32[]{:T(128)}, f32[8,192]{1,0:T(8,128)S(1)}, ...), condition=%wide.region_15.16_spmd, body=%wide.region_6.15_spmd.sunk | while | flops 823598080 | bytes 37431328 | solution.py:152
  64.0 2.1 fusion.153
  66.2 4.4 %conditional.4 = ((f32[8,192]{1,0:T(8,128)S(1)}, f32[8,192]{1,0:T(8,128)S(1)}, f32[8,192,128]{2,1,0:T(8,128)})) conditional(s32[]{:T(128)} %convert_element_type.402, (f32[8,192]{1,0:T(8,128)S(1)}, f32[8,192]{1,0:T(8,128)S(1)}, f32[8,192,128]{2,1,0:T(8,128)}) %tuple.74, (s32[]{:T(128)}, s32[192]{0:T(256)S(1)}, bf16[192,1024]{1,0:T(8,128)(2,1)S(1)}, ...), branch_computations={%region_7.7_spmd, %region_8.10_spmd} | conditional | flops 411799040 | bytes 18453340 | solution.py:143
  70.6 3.5 conditional.5
  75.3 2.1 fusion.153
  77.4 4.4 %conditional.4 = ((f32[8,192]{1,0:T(8,128)S(1)}, f32[8,192]{1,0:T(8,128)S(1)}, f32[8,192,128]{2,1,0:T(8,128)})) conditional(s32[]{:T(128)} %convert_element_type.402, (f32[8,192]{1,0:T(8,128)S(1)}, f32[8,192]{1,0:T(8,128)S(1)}, f32[8,192,128]{2,1,0:T(8,128)}) %tuple.74, (s32[]{:T(128)}, s32[192]{0:T(256)S(1)}, bf16[192,1024]{1,0:T(8,128)(2,1)S(1)}, ...), branch_computations={%region_7.7_spmd, %region_8.10_spmd} | conditional | flops 411799040 | bytes 18453340 | solution.py:143
  81.9 3.5 conditional.5
  86.6 2.1 fusion.153
  90.0 2.2 fusion.153
  93.5 2.1 fusion.153
  96.9 2.1 fusion.153
  100.3 2.1 fusion.153
  103.7 2.1 fusion.153
  107.1 2.1 fusion.153
  121.8 2.5 copy.163
  124.3 2.4 divide_convert_fusion
  126.7 4.6 %slice.72 = bf16[16,8,128,128]{2,1,3,0:T(8,128)(2,1)} slice(bf16[16,8,128,129]{2,1,3,0:T(8,128)(2,1)} %all-gather.8.cloned.1.call-done), slice={[0:16], [0:8], [0:128], [0:128]} | slice | bytes 8388608 | tf_op jit(solution)/shard_map/slice | solution.py:26
  131.2 6.7 %copy.225 = bf16[16,8,128,128]{3,2,1,0:T(8,128)(2,1)} copy(bf16[16,8,128,128]{2,1,3,0:T(8,128)(2,1)} %slice.72) | data formatting | bytes 8388608
  137.9 3.2 select_reduce_fusion
  147.3 2.8 fusion.128
  158.5 92.6 %all-gather.1 = bf16[128,128]{1,0:T(8,128)(2,1)S(1)} all-gather(bf16[8,128]{1,0:T(8,128)(2,1)S(1)} %add_convert_fusion), channel_id=3, replica_groups=mesh['seq'=16,'head'=16] {'seq'}, dimensions={0}, use_global_device_ids=true | all-gather | bytes 34816 | tf_op jit(solution)/shard_map/all_gather | solution.py:234
  251.1 4.7 %fusion.117 = f32[8,384,128]{2,1,0:T(8,128)S(1)} fusion(bf16[8,384,128]{2,1,0:T(8,128)(2,1)S(1)} %select_convert_fusion.2, f32[8,384,384]{1,2,0:T(8,128)} %copy-done.2), kind=kOutput, calls=%fused_computation.179 | convolution fusion | flops 306708480 | bytes 7077888 | tf_op jit(solution)/shard_map/hrs,hrf->hsf/dot_general | solution.py:49
  257.8 7.1 %all-gather.12.cloned.1.call-done = bf16[128,128,128]{2,1,0:T(8,128)(2,1)} async-done(((bf16[8,128,128]{2,1,0:T(8,128)(2,1)}), bf16[128,128,128]{2,1,0:T(8,128)(2,1)}) %all-gather.12.cloned.1.call-update) | async-done | bytes 4194320 | tf_op jit(solution)/shard_map/all_gather | solution.py:231
  264.9 3.2 fusion.48
  269.7 2.1 fusion.55
  274.1 54.6 %all-gather.14.cloned.1.call-done = bf16[4194304]{0:T(1024)(128)(2,1)} async-done(((bf16[262144]{0:T(1024)(128)(2,1)}), bf16[4194304]{0:T(1024)(128)(2,1)}) %all-gather.14.cloned.1.call-update) | async-done | bytes 8388624 | tf_op jit(solution)/shard_map/all_gather | solution.py:34
  328.7 7.6 %reshape.299 = bf16[16,262144]{1,0:T(8,128)(2,1)} reshape(bf16[4194304]{0:T(1024)(128)(2,1)} %all-gather.14.cloned.1.call-done) | data formatting | bytes 16777216 | tf_op jit(solution)/shard_map/all_gather | solution.py:34
  336.4 11.9 %reduce_sum.103 = bf16[262144]{0:T(1024)(128)(2,1)S(1)} reduce(bf16[16,262144]{1,0:T(8,128)(2,1)} %reshape.299, bf16[]{:T(256)} %constant.99.clone.1), dimensions={0}, to_apply=%region_19.20 | reduce | flops 3932160 | bytes 8912898 | tf_op jit(solution)/shard_map/reduce_sum | solution.py:34
  (183 shorter events, 56.5 us)
Async XLA Ops:
  7.2 10.8 %copy-start = (bf16[8,128,128]{2,1,0:T(8,128)(2,1)S(1)}, bf16[8,128,128]{2,1,0:T(8,128)(2,1)}, u32[]{:S(2)}) copy-start(bf16[8,128,128]{2,1,0:T(8,128)(2,1)} %param.15) | copy-start | bytes 786436
  7.2 9.3 %copy-start.5 = (bf16[384,1024]{1,0:T(8,128)(2,1)S(1)}, bf16[384,1024]{1,0:T(8,128)(2,1)}, u32[]{:S(2)}) copy-start(bf16[384,1024]{1,0:T(8,128)(2,1)} %param.11) | copy-start | bytes 2359300
  7.2 54.6 %all-gather.10.cloned.1.call-start = ((), (), s32[]{:S(2)}) async-start(), calls=%async_computation.1 | async-start | bytes 3342336 | tf_op jit(solution)/shard_map/all_gather | solution.py:116
  8.2 8.3 %copy-start.18 = (bf16[8,128,128]{2,1,0:T(8,128)(2,1)S(1)}, bf16[8,128,128]{2,1,0:T(8,128)(2,1)}, u32[]{:S(2)}) copy-start(bf16[8,128,128]{2,1,0:T(8,128)(2,1)} %param.14) | copy-start | bytes 786436
  9.3 5.5 %collective-permute-start = (bf16[2,384,64]{2,1,0:T(8,128)(2,1)S(1)}, bf16[2,384,64]{2,1,0:T(8,128)(2,1)S(1)}, u32[]{:S(2)}, u32[]{:S(2)}) collective-permute-start(bf16[2,384,64]{2,1,0:T(8,128)(2,1)S(1)} %pad_maximum_fusion.3), channel_id=1, source_target_pairs={{0,1},{1,0},{2,3},{3,2},{4,5},{5,4},{6,7},{7,6},{8,9},{9,8},{10,11... | collective-permute-start | bytes 294920 | tf_op jit(solution)/shard_map/ppermute | solution.py:18
  15.7 111.0 %all-gather.8.cloned.1.call-start = ((), (), s32[]{:S(2)}) async-start(), calls=%async_computation | async-start | bytes 4491264 | tf_op jit(solution)/shard_map/all_gather | solution.py:24
  17.0 2.2 copy-start.3
  17.0 1.1 copy-start.8
  19.2 1.2 copy-start.14
  19.2 2.2 copy-start.9
  21.2 243.7 %all-gather.12.cloned.1.call-start = ((), (), s32[]{:S(2)}) async-start(), calls=%async_computation.2 | async-start | bytes 4456448 | tf_op jit(solution)/shard_map/all_gather | solution.py:231
  67.1 1.1 copy-start.12
  69.7 0.9 copy-start.13
  78.4 1.2 copy-start.12
  81.0 0.9 copy-start.13
  119.5 0.9 copy-start.11
  141.8 2.4 copy-start.19
  142.2 1.9 copy-start.16
  142.3 1.9 copy-start.17
  147.0 181.7 %all-gather.14.cloned.1.call-start = ((), (), s32[]{:S(2)}) async-start(), calls=%async_computation.3 | async-start | bytes 8912896 | tf_op jit(solution)/shard_map/all_gather | solution.py:34
  150.8 1.1 copy-start.10
  152.0 2.1 copy-start.2
  152.0 2.5 copy-start.4
  154.5 1.7 copy-start.6
  156.2 99.7 %slice-start = ((s8[4718592]{0:T(1024)(128)(4,1)}), s8[524288]{0:T(1024)(128)(4,1)S(1)}, s32[]{:S(2)}) async-start(s8[4718592]{0:T(1024)(128)(4,1)} %bitcast.271), calls=%async_computation.4 | async-start | bytes 1048576
  158.2 97.7 %slice-start.1 = ((s8[4718592]{0:T(1024)(128)(4,1)}), s8[4194304]{0:T(1024)(128)(4,1)S(1)}, s32[]{:S(2)}) async-start(s8[4718592]{0:T(1024)(128)(4,1)} %bitcast.271), calls=%async_computation.5 | async-start | bytes 8388608
  268.3 1.4 copy-start.7
  272.3 1.0 copy-start.15
  336.4 13.7 %copy-start.1 = (bf16[8,128,128]{2,1,0:T(8,128)(2,1)S(1)}, bf16[8,128,128]{2,1,0:T(8,128)(2,1)}, u32[]{:S(2)}) copy-start(bf16[8,128,128]{2,1,0:T(8,128)(2,1)} %param.15) | copy-start | bytes 786436
Sparse Core Ops, SparseCore 0:
  15.8 45.9 all-gather.9
  63.7 40.6 all-gather.7
  147.1 117.7 all-gather.11
  274.2 54.4 all-gather.13
